TPU v7x, 32 devices: a whole 2x2x4 slice. The times are simulated.
32 devices in a mesh: dp: 16 (over z, y, x), inner: 2 (over core).
Axes of the slice: x: 2, y: 2, z: 4, core: 2. Of those that a mesh axis runs over, the one named last changes fastest.
Arguments:
- features: bfloat16 [8192, 2048], P(('dp', 'inner')), may hold values from -12 to 12
- kv_cotangent: bfloat16 [8192, 512], P(('dp', 'inner')), may hold values from -0.0625 to 0.0625
- owner_of_block: int32 [64], replicated, may hold values from 0 to 15, as said below
- first_moment: float32 [16, 4, 128, 128], P('dp'), may hold values from -1.25 to 1.25
- second_moment: float32 [16, 4, 128, 128], P('dp'), may hold values from 0.05 to 1
- left_stat: float32 [16, 4, 128, 128], P('dp')
- right_stat: float32 [16, 4, 128, 128], P('dp')
- left_basis: bfloat16 [16, 4, 128, 128], P('dp')
- right_basis: bfloat16 [16, 4, 128, 128], P('dp')
Outputs:
- update: bfloat16 [2048, 512], replicated
- new_left_basis: bfloat16 [16, 4, 128, 128], P('dp')
- new_right_basis: bfloat16 [16, 4, 128, 128], P('dp')
Inputs may be any that keep to these rules, and one draw needn't show every extreme that they name: `owner_of_block`: each index of dp owns at most 4 tiles, and one index owns exactly 4.
All inputs are finite; a program needn't handle non-finite values.
Results may differ from a plain program's by a relative error of at most 0.001.
Values may be sent and summed in bfloat16 or wider, within the bound.
No kernel may reach another device: no remote copies, remote signals or barrier semaphores. Data moves between devices by JAX's collectives and lax.ppermute only.
A program may use at most 64 MiB of HBM per device.

v0:
```python
import jax
import jax.numpy as jnp
from jax import lax
from jax.sharding import PartitionSpec as P

NS_STEPS = 12
highest = lax.Precision.HIGHEST


def rotate_in(basis_left, matrix, basis_right):
    half = jnp.einsum("sji,sjk->sik", basis_left, matrix, precision=highest)
    return jnp.einsum("sij,sjk->sik", half, basis_right, precision=highest)


def rotate_out(basis_left, matrix, basis_right):
    half = jnp.einsum("sij,sjk->sik", basis_left, matrix, precision=highest)
    return jnp.einsum("sij,skj->sik", half, basis_right, precision=highest)


def orthogonalize(stat, basis):
    power = jnp.einsum("sij,sjk->sik", stat, basis, precision=highest)
    scale = jnp.sqrt(jnp.sum(power * power, axis=(1, 2), keepdims=True) + 1e-06)
    iterate = power / scale
    for sweep in range(NS_STEPS):
        gram = jnp.einsum("sji,sjk->sik", iterate, iterate, precision=highest)
        iterate = 1.5 * iterate - 0.5 * jnp.einsum("sij,sjk->sik", iterate, gram, precision=highest)
    return iterate


def soap_tiles(grads, first, second, stat_left, stat_right, basis_left, basis_right):
    rotated = rotate_in(basis_left, grads, basis_right)
    moment = 0.95 * first + 0.05 * grads
    moment_rot = rotate_in(basis_left, moment, basis_right)
    second_new = 0.95 * second + 0.05 * rotated * rotated
    direction = rotate_out(basis_left, moment_rot / (jnp.sqrt(second_new) + 1e-08), basis_right)
    left_new = 0.95 * stat_left + 0.05 * jnp.einsum("sij,skj->sik", grads, grads, precision=highest)
    right_new = 0.95 * stat_right + 0.05 * jnp.einsum(
        "sji,sjk->sik", grads, grads, precision=highest
    )
    return (direction, orthogonalize(left_new, basis_left), orthogonalize(right_new, basis_right))


def per_device(
    features,
    kv_cotangent,
    owner_of_block,
    first_moment,
    second_moment,
    left_stat,
    right_stat,
    left_basis,
    right_basis,
):
    tile = left_basis.shape[-1]
    capacity = left_basis.shape[1]
    d_win = features.shape[1]
    width = kv_cotangent.shape[1]
    row_tiles = d_win // tile
    col_tiles = width // tile
    nblocks = owner_of_block.shape[0]
    owner_here = lax.axis_index("dp")
    block_ids = jnp.arange(nblocks, dtype=jnp.int32)
    same = owner_of_block[:, None] == owner_of_block[None, :]
    earlier = block_ids[None, :] < block_ids[:, None]
    slot = jnp.sum((same & earlier).astype(jnp.int32), axis=1)
    slot_ids = jnp.arange(capacity, dtype=jnp.int32)
    match = (owner_of_block[None, :] == owner_here) & (slot[None, :] == slot_ids[:, None])
    live = jnp.any(match, axis=1)
    which = jnp.sum(jnp.where(match, block_ids[None, :], 0), axis=1)
    row_start = which // col_tiles * tile
    col_start = which % col_tiles * tile
    partial_grad = lax.dot_general(
        features, kv_cotangent, (((0,), (0,)), ((), ())), preferred_element_type=jnp.float32
    )
    grad = lax.psum(partial_grad, ("dp", "inner"))
    fetched = [
        lax.dynamic_slice(grad, (row_start[slot_index], col_start[slot_index]), (tile, tile))
        for slot_index in range(capacity)
    ]
    grads = jnp.stack(fetched)
    basis_left = left_basis[0].astype(jnp.float32)
    basis_right = right_basis[0].astype(jnp.float32)
    direction, left_iter, right_iter = soap_tiles(
        grads,
        first_moment[0],
        second_moment[0],
        left_stat[0],
        right_stat[0],
        basis_left,
        basis_right,
    )
    direction_low = direction.astype(jnp.bfloat16)
    everyone = lax.all_gather(direction_low[None], "dp", axis=0, tiled=True)
    tiles = everyone[owner_of_block, slot]
    update = (
        tiles.reshape(row_tiles, col_tiles, tile, tile).transpose(0, 2, 1, 3).reshape(d_win, width)
    )
    keep = live[:, None, None]
    new_left = jnp.where(keep, left_iter.astype(jnp.bfloat16), left_basis[0])
    new_right = jnp.where(keep, right_iter.astype(jnp.bfloat16), right_basis[0])
    return (update, new_left[None], new_right[None])


def solution(mesh):
    return jax.shard_map(
        per_device,
        mesh=mesh,
        in_specs=(
            P(("dp", "inner"), None),
            P(("dp", "inner"), None),
            P(),
            P("dp", None, None, None),
            P("dp", None, None, None),
            P("dp", None, None, None),
            P("dp", None, None, None),
            P("dp", None, None, None),
            P("dp", None, None, None),
        ),
        out_specs=(P(), P("dp", None, None, None), P("dp", None, None, None)),
        check_vma=False,
    )
```

profile of v0, /device:TPU:0, one launch (start us, length us, event | category | flops | bytes accessed | tf_op | source)
XLA Modules:
  0.0 234.5 jit_solution(13853577143957279118)
XLA Ops:
  7.2 1.2 copy-done
  8.4 3.6 %fusion.71 = f32[2048,512]{1,0:T(8,128)} fusion(bf16[256,2048]{1,0:T(8,128)(2,1)S(1)} %copy-done, bf16[256,512]{1,0:T(8,128)(2,1)} %param.10), kind=kOutput, calls=%fused_computation.126 | convolution fusion | flops 536870912 | bytes 5505024 | tf_op jit(solution)/shard_map/dot_general | solution.py:72
  13.0 0.7 fusion.69
  28.8 129.2 %all-reduce.2.cloned.1.call-done = f32[2048,512]{1,0:T(8,128)} async-done(((f32[2048,512]{1,0:T(8,128)}), f32[2048,512]{1,0:T(8,128)}) %all-reduce.2.cloned.1.call-update) | async-done | bytes 4194320 | tf_op jit(solution)/shard_map/psum | solution.py:75
  158.0 1.1 dynamic-slice_bitcast_fusion.3
  160.7 1.0 convolution_convert_fusion
  161.8 0.7 fusion.25
  162.8 0.7 fusion.53
  164.0 0.6 fusion.72
  165.0 0.6 fusion.73
  166.0 0.6 fusion.74
  168.1 0.6 fusion.76
  169.1 0.6 fusion.77
  170.1 0.6 fusion.78
  171.1 0.6 fusion.79
  172.1 0.6 fusion.80
  174.4 0.6 fusion.82
  175.0 0.6 fusion.12
  175.9 0.7 fusion.54
  178.1 0.6 fusion.84
  179.1 0.6 fusion.85
  180.1 1.1 fusion.31
  182.2 0.6 fusion.87
  183.3 0.6 fusion.88
  184.3 0.6 fusion.89
  185.3 0.6 fusion.90
  187.3 0.8 fusion.92
  189.2 1.1 fusion.29
  190.3 31.4 %all-gather.3.cloned.1.call-done = bf16[64,128,128]{2,1,0:T(8,128)(2,1)} async-done(((bf16[4,128,128]{2,1,0:T(8,128)(2,1)}), bf16[64,128,128]{2,1,0:T(8,128)(2,1)}) %all-gather.3.cloned.1.call-update) | async-done | bytes 2097168 | tf_op jit(solution)/shard_map/all_gather | solution.py:93
  221.7 2.5 %gather_fusion = bf16[64,128,128]{2,1,0:T(8,128)(2,1)S(1)} fusion(bf16[16,4,128,128]{3,2,1,0:T(8,128)(2,1)} %bitcast.173, s32[64]{0:T(128)S(1)} %fusion.65), kind=kCustom, calls=%fused_computation | custom fusion | bytes 4194816 | tf_op jit(solution)/shard_map/gather | solution.py:94
  224.2 1.8 copy.20
  226.0 1.7 copy.79
  (62 shorter events, 16.1 us)
Async XLA Ops:
  7.2 1.2 copy-start
  7.2 150.8 %all-reduce.2.cloned.1.call-start = ((), (), s32[]{:S(2)}) async-start(), calls=%async_computation | async-start | bytes 8388608 | tf_op jit(solution)/shard_map/psum | solution.py:75
  12.0 0.7 copy-start.7
  12.0 147.1 %copy-start.1 = (bf16[1,4,128,128]{3,2,1,0:T(8,128)(2,1)S(1)}, bf16[1,4,128,128]{3,2,1,0:T(8,128)(2,1)}, u32[]{:S(2)}) copy-start(bf16[1,4,128,128]{3,2,1,0:T(8,128)(2,1)} %param.16) | copy-start | bytes 393220
  12.0 147.5 %copy-start.3 = (f32[1,4,128,128]{3,2,1,0:T(8,128)S(1)}, f32[1,4,128,128]{3,2,1,0:T(8,128)}, u32[]{:S(2)}) copy-start(f32[1,4,128,128]{3,2,1,0:T(8,128)} %param.12) | copy-start | bytes 786436
  12.1 147.8 %copy-start.2 = (bf16[1,4,128,128]{3,2,1,0:T(8,128)(2,1)S(1)}, bf16[1,4,128,128]{3,2,1,0:T(8,128)(2,1)}, u32[]{:S(2)}) copy-start(bf16[1,4,128,128]{3,2,1,0:T(8,128)(2,1)} %param.17) | copy-start | bytes 393220
  12.1 148.0 %copy-start.6 = (f32[1,4,128,128]{3,2,1,0:T(8,128)S(1)}, f32[1,4,128,128]{3,2,1,0:T(8,128)}, u32[]{:S(2)}) copy-start(f32[1,4,128,128]{3,2,1,0:T(8,128)} %param.13) | copy-start | bytes 786436
  12.1 209.6 %all-gather.3.cloned.1.call-start = ((), (), s32[]{:S(2)}) async-start(), calls=%async_computation.1 | async-start | bytes 2228224 | tf_op jit(solution)/shard_map/all_gather | solution.py:93
  159.5 2.3 copy-start.4
  172.1 2.8 %copy-start.5 = (f32[1,4,128,128]{3,2,1,0:T(8,128)S(1)}, f32[1,4,128,128]{3,2,1,0:T(8,128)}, u32[]{:S(2)}) copy-start(f32[1,4,128,128]{3,2,1,0:T(8,128)} %param.15) | copy-start | bytes 786436
Sparse Core Ops, SparseCore 0:
  13.5 144.4 all-reduce.1
  161.9 59.6 all-gather.2
where the time goes:
time: 235 us
  waiting for transfers between devices  161 us (69%)
  matrix products  34.2 us (15%)
  between operations  29.5 us (13%)
  local copies, waits for them, and re-layouts  9.58 us (4%)
    psum x1, waiting for transfers between devices, per_device(): grad = lax.psum(partial_grad, ('dp', 'inner'))  129 us
    all_gather x1, waiting for transfers between devices, per_device(): everyone = lax.all_gather(direction_low[None], 'dp', axis=0, tiled=True)  31.4 us
    dot_general x24, matrix products, orthogonalize(): gram = jnp.einsum('sji,sjk->sik', iterate, iterate, precision=highest)  14.8 us
    dot_general x24, matrix products, orthogonalize(): jnp.einsum('sij,sjk->sik', iterate, gram, precision=highest)  11.3 us
  transfers between devices with their start and end apart: 2, of which 2 were waited for; matrix products, arithmetic and copies ran while one was open for 12% of the time, Pallas kernels for 0%

commit v1 on v0

--- a/solution.py
+++ b/solution.py
@@ -5,6 +5,22 @@
 
 NS_STEPS = 12
 highest = lax.Precision.HIGHEST
+
+
+def ring_gather(x, axis, dim):
+    ways, here, step = (lax.axis_size(axis), lax.axis_index(axis), x.shape[dim])
+    shape = [n * ways if d == dim else n for d, n in enumerate(x.shape)]
+    full = lax.dynamic_update_slice_in_dim(jnp.zeros(shape, x.dtype), x, here * step, axis=dim)
+    going_up = going_down = x
+    for far in range(1, ways // 2 + 1):
+        going_up = lax.ppermute(going_up, axis, [(d, (d + 1) % ways) for d in range(ways)])
+        full = lax.dynamic_update_slice_in_dim(full, going_up, (here - far) % ways * step, axis=dim)
+        if 2 * far < ways:
+            going_down = lax.ppermute(going_down, axis, [(d, (d - 1) % ways) for d in range(ways)])
+            full = lax.dynamic_update_slice_in_dim(
+                full, going_down, (here + far) % ways * step, axis=dim
+            )
+    return full
 
 
 def rotate_in(basis_left, matrix, basis_right):
@@ -90,7 +106,7 @@
         basis_right,
     )
     direction_low = direction.astype(jnp.bfloat16)
-    everyone = lax.all_gather(direction_low[None], "dp", axis=0, tiled=True)
+    everyone = ring_gather(direction_low[None], "dp", 0)
     tiles = everyone[owner_of_block, slot]
     update = (
         tiles.reshape(row_tiles, col_tiles, tile, tile).transpose(0, 2, 1, 3).reshape(d_win, width)

time: 235 us -> 272 us (1.16)
  starting transfers between devices: 0.08 us -> 39.9 us
  waiting for transfers between devices: 161 us -> 157 us
    ppermute x0 -> x15, starting transfers between devices: none -> 39.8 us  [the longest x7 38.2 us: ring_gather(): lax.ppermute(going_down, axis, [(d, (d - 1) % ways) for d in range(ways)])]
    all_gather x1 -> x0, waiting for transfers between devices: 31.4 us -> none  [per_device(): everyone = lax.all_gather(direction_low[None], 'dp', axis=0, tiled=True)]
    ppermute x0 -> x15, waiting for transfers between devices: none -> 27.5 us  [the longest x8 27.5 us: ring_gather(): lax.ppermute(going_up, axis, [(d, (d + 1) % ways) for d in range(ways)])]
    unnamed x17 -> x18, local copies, waits for them, and re-layouts: 3.44 us -> 6.85 us
  transfers between devices with their start and end apart: 2 -> 16, of which waited for: 2 -> 8; matrix products, arithmetic and copies ran while one was open for 12% -> 11% of each run, Pallas kernels for 0% -> 0%
where the time goes in v1:
time: 272 us
  waiting for transfers between devices  157 us (58%)
  starting transfers between devices  39.9 us (15%)
  matrix products  33.3 us (12%)
  between operations  29.6 us (11%)
  local copies, waits for them, and re-layouts  11.6 us (4%)
    psum x1, waiting for transfers between devices, per_device(): grad = lax.psum(partial_grad, ('dp', 'inner'))  129 us
    ppermute x7, starting transfers between devices, ring_gather(): lax.ppermute(going_down, axis, [(d, (d - 1) % ways) for d in range(ways)])  38.2 us
    ppermute x8, waiting for transfers between devices, ring_gather(): lax.ppermute(going_up, axis, [(d, (d + 1) % ways) for d in range(ways)])  27.5 us
    dot_general x24, matrix products, orthogonalize(): gram = jnp.einsum('sji,sjk->sik', iterate, iterate, precision=highest)  14.5 us
    dot_general x24, matrix products, orthogonalize(): jnp.einsum('sij,sjk->sik', iterate, gram, precision=highest)  11.1 us
    unnamed x18, local copies, waits for them, and re-layouts  6.85 us
  transfers between devices with their start and end apart: 16, of which 8 were waited for; matrix products, arithmetic and copies ran while one was open for 11% of the time, Pallas kernels for 0%

profile of v1, /device:TPU:0, one launch (start us, length us, event | category | flops | bytes accessed | tf_op | source)
XLA Modules:
  0.0 271.7 jit_solution(17220127413089115059)
XLA Ops:
  7.2 1.2 copy-done
  8.4 3.7 %fusion.72 = f32[2048,512]{1,0:T(8,128)} fusion(bf16[256,2048]{1,0:T(8,128)(2,1)S(1)} %copy-done, bf16[256,512]{1,0:T(8,128)(2,1)} %param.10), kind=kOutput, calls=%fused_computation.143 | convolution fusion | flops 536870912 | bytes 5505024 | tf_op jit(solution)/shard_map/dot_general | solution.py:88
  13.0 0.6 fusion.70
  28.7 129.3 %all-reduce.2.cloned.1.call-done = f32[2048,512]{1,0:T(8,128)} async-done(((f32[2048,512]{1,0:T(8,128)}), f32[2048,512]{1,0:T(8,128)}) %all-reduce.2.cloned.1.call-update) | async-done | bytes 4194320 | tf_op jit(solution)/shard_map/psum | solution.py:91
  158.0 1.1 dynamic-slice_bitcast_fusion.3
  161.6 1.6 collective-permute-start
  163.2 4.1 %collective-permute-start.1 = (bf16[1,4,128,128]{3,2,1,0:T(8,128)(2,1)S(1)}, bf16[1,4,128,128]{3,2,1,0:T(8,128)(2,1)S(1)}, u32[]{:S(2)}, u32[]{:S(2)}) collective-permute-start(bf16[1,4,128,128]{3,2,1,0:T(8,128)(2,1)S(1)} %get-tuple-element.24), channel_id=1, source_target_pairs={{0,30},{2,0},{4,2},{6,4},{8,6},{10,8},{12,10},{14,12},{16,14},{18,... | collective-permute-start | bytes 393224 | tf_op jit(solution)/shard_map/ppermute | solution.py:19
  167.3 0.6 fusion.12
  168.3 0.7 fusion.55
  169.4 0.6 fusion.84
  171.5 0.6 fusion.86
  172.5 0.6 fusion.87
  180.2 0.9 fusion.25
  181.5 0.7 fusion.54
  193.4 1.1 fusion.30
  194.5 1.1 fusion.32
  195.6 5.6 %collective-permute-start.3 = (bf16[1,4,128,128]{3,2,1,0:T(8,128)(2,1)S(1)}, bf16[1,4,128,128]{3,2,1,0:T(8,128)(2,1)S(1)}, u32[]{:S(2)}, u32[]{:S(2)}) collective-permute-start(bf16[1,4,128,128]{3,2,1,0:T(8,128)(2,1)S(1)} %collective-permute-done.1), channel_id=1, source_target_pairs={{0,30},{2,0},{4,2},{6,4},{8,6},{10,8},{12,10},{14,12},{16,14},{18,... | collective-permute-start | bytes 393224 | tf_op jit(solution)/shard_map/ppermute | solution.py:19
  201.2 2.9 %collective-permute-done.2 = bf16[1,4,128,128]{3,2,1,0:T(8,128)(2,1)S(1)} collective-permute-done((bf16[1,4,128,128]{3,2,1,0:T(8,128)(2,1)S(1)}, bf16[1,4,128,128]{3,2,1,0:T(8,128)(2,1)S(1)}, u32[]{:S(2)}, u32[]{:S(2)}) %collective-permute-start.2) | collective-permute-done | bytes 131104 | tf_op jit(solution)/shard_map/ppermute | solution.py:16
  204.1 5.7 %collective-permute-start.5 = (bf16[1,4,128,128]{3,2,1,0:T(8,128)(2,1)S(1)}, bf16[1,4,128,128]{3,2,1,0:T(8,128)(2,1)S(1)}, u32[]{:S(2)}, u32[]{:S(2)}) collective-permute-start(bf16[1,4,128,128]{3,2,1,0:T(8,128)(2,1)S(1)} %collective-permute-done.3), channel_id=1, source_target_pairs={{0,30},{2,0},{4,2},{6,4},{8,6},{10,8},{12,10},{14,12},{16,14},{18,... | collective-permute-start | bytes 393224 | tf_op jit(solution)/shard_map/ppermute | solution.py:19
  209.9 2.8 %collective-permute-done.4 = bf16[1,4,128,128]{3,2,1,0:T(8,128)(2,1)S(1)} collective-permute-done((bf16[1,4,128,128]{3,2,1,0:T(8,128)(2,1)S(1)}, bf16[1,4,128,128]{3,2,1,0:T(8,128)(2,1)S(1)}, u32[]{:S(2)}, u32[]{:S(2)}) %collective-permute-start.4) | collective-permute-done | bytes 131104 | tf_op jit(solution)/shard_map/ppermute | solution.py:16
  212.7 5.7 %collective-permute-start.7 = (bf16[1,4,128,128]{3,2,1,0:T(8,128)(2,1)S(1)}, bf16[1,4,128,128]{3,2,1,0:T(8,128)(2,1)S(1)}, u32[]{:S(2)}, u32[]{:S(2)}) collective-permute-start(bf16[1,4,128,128]{3,2,1,0:T(8,128)(2,1)S(1)} %collective-permute-done.5), channel_id=1, source_target_pairs={{0,30},{2,0},{4,2},{6,4},{8,6},{10,8},{12,10},{14,12},{16,14},{18,... | collective-permute-start | bytes 393224 | tf_op jit(solution)/shard_map/ppermute | solution.py:19
  218.5 2.9 %collective-permute-done.6 = bf16[1,4,128,128]{3,2,1,0:T(8,128)(2,1)S(1)} collective-permute-done((bf16[1,4,128,128]{3,2,1,0:T(8,128)(2,1)S(1)}, bf16[1,4,128,128]{3,2,1,0:T(8,128)(2,1)S(1)}, u32[]{:S(2)}, u32[]{:S(2)}) %collective-permute-start.6) | collective-permute-done | bytes 131104 | tf_op jit(solution)/shard_map/ppermute | solution.py:16
  221.4 5.6 %collective-permute-start.9 = (bf16[1,4,128,128]{3,2,1,0:T(8,128)(2,1)S(1)}, bf16[1,4,128,128]{3,2,1,0:T(8,128)(2,1)S(1)}, u32[]{:S(2)}, u32[]{:S(2)}) collective-permute-start(bf16[1,4,128,128]{3,2,1,0:T(8,128)(2,1)S(1)} %collective-permute-done.7), channel_id=1, source_target_pairs={{0,30},{2,0},{4,2},{6,4},{8,6},{10,8},{12,10},{14,12},{16,14},{18,... | collective-permute-start | bytes 393224 | tf_op jit(solution)/shard_map/ppermute | solution.py:19
  227.1 3.7 %collective-permute-done.8 = bf16[1,4,128,128]{3,2,1,0:T(8,128)(2,1)S(1)} collective-permute-done((bf16[1,4,128,128]{3,2,1,0:T(8,128)(2,1)S(1)}, bf16[1,4,128,128]{3,2,1,0:T(8,128)(2,1)S(1)}, u32[]{:S(2)}, u32[]{:S(2)}) %collective-permute-start.8) | collective-permute-done | bytes 131104 | tf_op jit(solution)/shard_map/ppermute | solution.py:16
  230.8 5.9 %collective-permute-start.11 = (bf16[1,4,128,128]{3,2,1,0:T(8,128)(2,1)S(1)}, bf16[1,4,128,128]{3,2,1,0:T(8,128)(2,1)S(1)}, u32[]{:S(2)}, u32[]{:S(2)}) collective-permute-start(bf16[1,4,128,128]{3,2,1,0:T(8,128)(2,1)S(1)} %collective-permute-done.9), channel_id=1, source_target_pairs={{0,30},{2,0},{4,2},{6,4},{8,6},{10,8},{12,10},{14,12},{16,14},{18,... | collective-permute-start | bytes 393224 | tf_op jit(solution)/shard_map/ppermute | solution.py:19
  236.7 3.7 %collective-permute-done.10 = bf16[1,4,128,128]{3,2,1,0:T(8,128)(2,1)S(1)} collective-permute-done((bf16[1,4,128,128]{3,2,1,0:T(8,128)(2,1)S(1)}, bf16[1,4,128,128]{3,2,1,0:T(8,128)(2,1)S(1)}, u32[]{:S(2)}, u32[]{:S(2)}) %collective-permute-start.10) | collective-permute-done | bytes 131104 | tf_op jit(solution)/shard_map/ppermute | solution.py:16
  240.4 5.6 %collective-permute-start.13 = (bf16[1,4,128,128]{3,2,1,0:T(8,128)(2,1)S(1)}, bf16[1,4,128,128]{3,2,1,0:T(8,128)(2,1)S(1)}, u32[]{:S(2)}, u32[]{:S(2)}) collective-permute-start(bf16[1,4,128,128]{3,2,1,0:T(8,128)(2,1)S(1)} %collective-permute-done.11), channel_id=1, source_target_pairs={{0,30},{2,0},{4,2},{6,4},{8,6},{10,8},{12,10},{14,12},{16,14},{18,... | collective-permute-start | bytes 393224 | tf_op jit(solution)/shard_map/ppermute | solution.py:19
  246.1 3.0 %collective-permute-done.12 = bf16[1,4,128,128]{3,2,1,0:T(8,128)(2,1)S(1)} collective-permute-done((bf16[1,4,128,128]{3,2,1,0:T(8,128)(2,1)S(1)}, bf16[1,4,128,128]{3,2,1,0:T(8,128)(2,1)S(1)}, u32[]{:S(2)}, u32[]{:S(2)}) %collective-permute-start.12) | collective-permute-done | bytes 131104 | tf_op jit(solution)/shard_map/ppermute | solution.py:16
  249.1 8.5 %collective-permute-done.14 = bf16[1,4,128,128]{3,2,1,0:T(8,128)(2,1)S(1)} collective-permute-done((bf16[1,4,128,128]{3,2,1,0:T(8,128)(2,1)S(1)}, bf16[1,4,128,128]{3,2,1,0:T(8,128)(2,1)S(1)}, u32[]{:S(2)}, u32[]{:S(2)}) %collective-permute-start.14) | collective-permute-done | bytes 131104 | tf_op jit(solution)/shard_map/ppermute | solution.py:16
  257.6 2.1 gather_fusion
  259.8 3.4 %copy.109 = bf16[16,128,4,128]{3,2,1,0:T(4,128)(2,1)S(1)} copy(bf16[16,128,4,128]{3,1,2,0:T(8,128)(2,1)} %bitcast.175) | data formatting | bytes 4194304
  263.2 1.7 copy.113
  (105 shorter events, 24.9 us)
Async XLA Ops:
  7.2 1.2 copy-start
  7.2 150.8 %all-reduce.2.cloned.1.call-start = ((), (), s32[]{:S(2)}) async-start(), calls=%async_computation | async-start | bytes 8388608 | tf_op jit(solution)/shard_map/psum | solution.py:91
  12.1 0.7 copy-start.7
  12.1 147.1 %copy-start.1 = (bf16[1,4,128,128]{3,2,1,0:T(8,128)(2,1)S(1)}, bf16[1,4,128,128]{3,2,1,0:T(8,128)(2,1)}, u32[]{:S(2)}) copy-start(bf16[1,4,128,128]{3,2,1,0:T(8,128)(2,1)} %param.16) | copy-start | bytes 393220
  12.1 147.5 %copy-start.3 = (f32[1,4,128,128]{3,2,1,0:T(8,128)S(1)}, f32[1,4,128,128]{3,2,1,0:T(8,128)}, u32[]{:S(2)}) copy-start(f32[1,4,128,128]{3,2,1,0:T(8,128)} %param.12) | copy-start | bytes 786436
  12.1 147.8 %copy-start.2 = (bf16[1,4,128,128]{3,2,1,0:T(8,128)(2,1)S(1)}, bf16[1,4,128,128]{3,2,1,0:T(8,128)(2,1)}, u32[]{:S(2)}) copy-start(bf16[1,4,128,128]{3,2,1,0:T(8,128)(2,1)} %param.17) | copy-start | bytes 393220
  12.1 148.0 %copy-start.6 = (f32[1,4,128,128]{3,2,1,0:T(8,128)S(1)}, f32[1,4,128,128]{3,2,1,0:T(8,128)}, u32[]{:S(2)}) copy-start(f32[1,4,128,128]{3,2,1,0:T(8,128)} %param.13) | copy-start | bytes 786436
  160.1 7.2 %copy-start.4 = (f32[1,4,128,128]{3,2,1,0:T(8,128)S(1)}, f32[1,4,128,128]{3,2,1,0:T(8,128)}, u32[]{:S(2)}) copy-start(f32[1,4,128,128]{3,2,1,0:T(8,128)} %param.15) | copy-start | bytes 786436
  161.6 33.9 %collective-permute-start = (bf16[1,4,128,128]{3,2,1,0:T(8,128)(2,1)S(1)}, bf16[1,4,128,128]{3,2,1,0:T(8,128)(2,1)S(1)}, u32[]{:S(2)}, u32[]{:S(2)}) collective-permute-start(bf16[1,4,128,128]{3,2,1,0:T(8,128)(2,1)S(1)} %get-tuple-element.24), channel_id=1, source_target_pairs={{0,2},{2,4},{4,6},{6,8},{8,10},{10,12},{12,14},{14,16},{16,18},{18... | collective-permute-start | bytes 393224 | tf_op jit(solution)/shard_map/ppermute | solution.py:16
  163.2 32.3 %collective-permute-start.1 = (bf16[1,4,128,128]{3,2,1,0:T(8,128)(2,1)S(1)}, bf16[1,4,128,128]{3,2,1,0:T(8,128)(2,1)S(1)}, u32[]{:S(2)}, u32[]{:S(2)}) collective-permute-start(bf16[1,4,128,128]{3,2,1,0:T(8,128)(2,1)S(1)} %get-tuple-element.24), channel_id=1, source_target_pairs={{0,30},{2,0},{4,2},{6,4},{8,6},{10,8},{12,10},{14,12},{16,14},{18,... | collective-permute-start | bytes 393224 | tf_op jit(solution)/shard_map/ppermute | solution.py:19
  177.6 2.7 copy-start.5
  195.6 8.6 %collective-permute-start.2 = (bf16[1,4,128,128]{3,2,1,0:T(8,128)(2,1)S(1)}, bf16[1,4,128,128]{3,2,1,0:T(8,128)(2,1)S(1)}, u32[]{:S(2)}, u32[]{:S(2)}) collective-permute-start(bf16[1,4,128,128]{3,2,1,0:T(8,128)(2,1)S(1)} %collective-permute-done), channel_id=1, source_target_pairs={{0,2},{2,4},{4,6},{6,8},{8,10},{10,12},{12,14},{14,16},{16,18},{18... | collective-permute-start | bytes 393224 | tf_op jit(solution)/shard_map/ppermute | solution.py:16
  195.6 8.6 %collective-permute-start.3 = (bf16[1,4,128,128]{3,2,1,0:T(8,128)(2,1)S(1)}, bf16[1,4,128,128]{3,2,1,0:T(8,128)(2,1)S(1)}, u32[]{:S(2)}, u32[]{:S(2)}) collective-permute-start(bf16[1,4,128,128]{3,2,1,0:T(8,128)(2,1)S(1)} %collective-permute-done.1), channel_id=1, source_target_pairs={{0,30},{2,0},{4,2},{6,4},{8,6},{10,8},{12,10},{14,12},{16,14},{18,... | collective-permute-start | bytes 393224 | tf_op jit(solution)/shard_map/ppermute | solution.py:19
  204.1 8.6 %collective-permute-start.4 = (bf16[1,4,128,128]{3,2,1,0:T(8,128)(2,1)S(1)}, bf16[1,4,128,128]{3,2,1,0:T(8,128)(2,1)S(1)}, u32[]{:S(2)}, u32[]{:S(2)}) collective-permute-start(bf16[1,4,128,128]{3,2,1,0:T(8,128)(2,1)S(1)} %collective-permute-done.2), channel_id=1, source_target_pairs={{0,2},{2,4},{4,6},{6,8},{8,10},{10,12},{12,14},{14,16},{16,18},{18... | collective-permute-start | bytes 393224 | tf_op jit(solution)/shard_map/ppermute | solution.py:16
  204.1 8.6 %collective-permute-start.5 = (bf16[1,4,128,128]{3,2,1,0:T(8,128)(2,1)S(1)}, bf16[1,4,128,128]{3,2,1,0:T(8,128)(2,1)S(1)}, u32[]{:S(2)}, u32[]{:S(2)}) collective-permute-start(bf16[1,4,128,128]{3,2,1,0:T(8,128)(2,1)S(1)} %collective-permute-done.3), channel_id=1, source_target_pairs={{0,30},{2,0},{4,2},{6,4},{8,6},{10,8},{12,10},{14,12},{16,14},{18,... | collective-permute-start | bytes 393224 | tf_op jit(solution)/shard_map/ppermute | solution.py:19
  212.7 8.7 %collective-permute-start.6 = (bf16[1,4,128,128]{3,2,1,0:T(8,128)(2,1)S(1)}, bf16[1,4,128,128]{3,2,1,0:T(8,128)(2,1)S(1)}, u32[]{:S(2)}, u32[]{:S(2)}) collective-permute-start(bf16[1,4,128,128]{3,2,1,0:T(8,128)(2,1)S(1)} %collective-permute-done.4), channel_id=1, source_target_pairs={{0,2},{2,4},{4,6},{6,8},{8,10},{10,12},{12,14},{14,16},{16,18},{18... | collective-permute-start | bytes 393224 | tf_op jit(solution)/shard_map/ppermute | solution.py:16
  212.7 8.7 %collective-permute-start.7 = (bf16[1,4,128,128]{3,2,1,0:T(8,128)(2,1)S(1)}, bf16[1,4,128,128]{3,2,1,0:T(8,128)(2,1)S(1)}, u32[]{:S(2)}, u32[]{:S(2)}) collective-permute-start(bf16[1,4,128,128]{3,2,1,0:T(8,128)(2,1)S(1)} %collective-permute-done.5), channel_id=1, source_target_pairs={{0,30},{2,0},{4,2},{6,4},{8,6},{10,8},{12,10},{14,12},{16,14},{18,... | collective-permute-start | bytes 393224 | tf_op jit(solution)/shard_map/ppermute | solution.py:19
  221.4 9.4 %collective-permute-start.8 = (bf16[1,4,128,128]{3,2,1,0:T(8,128)(2,1)S(1)}, bf16[1,4,128,128]{3,2,1,0:T(8,128)(2,1)S(1)}, u32[]{:S(2)}, u32[]{:S(2)}) collective-permute-start(bf16[1,4,128,128]{3,2,1,0:T(8,128)(2,1)S(1)} %collective-permute-done.6), channel_id=1, source_target_pairs={{0,2},{2,4},{4,6},{6,8},{8,10},{10,12},{12,14},{14,16},{16,18},{18... | collective-permute-start | bytes 393224 | tf_op jit(solution)/shard_map/ppermute | solution.py:16
  221.4 9.4 %collective-permute-start.9 = (bf16[1,4,128,128]{3,2,1,0:T(8,128)(2,1)S(1)}, bf16[1,4,128,128]{3,2,1,0:T(8,128)(2,1)S(1)}, u32[]{:S(2)}, u32[]{:S(2)}) collective-permute-start(bf16[1,4,128,128]{3,2,1,0:T(8,128)(2,1)S(1)} %collective-permute-done.7), channel_id=1, source_target_pairs={{0,30},{2,0},{4,2},{6,4},{8,6},{10,8},{12,10},{14,12},{16,14},{18,... | collective-permute-start | bytes 393224 | tf_op jit(solution)/shard_map/ppermute | solution.py:19
  230.8 9.6 %collective-permute-start.10 = (bf16[1,4,128,128]{3,2,1,0:T(8,128)(2,1)S(1)}, bf16[1,4,128,128]{3,2,1,0:T(8,128)(2,1)S(1)}, u32[]{:S(2)}, u32[]{:S(2)}) collective-permute-start(bf16[1,4,128,128]{3,2,1,0:T(8,128)(2,1)S(1)} %collective-permute-done.8), channel_id=1, source_target_pairs={{0,2},{2,4},{4,6},{6,8},{8,10},{10,12},{12,14},{14,16},{16,18},{18... | collective-permute-start | bytes 393224 | tf_op jit(solution)/shard_map/ppermute | solution.py:16
  230.8 9.6 %collective-permute-start.11 = (bf16[1,4,128,128]{3,2,1,0:T(8,128)(2,1)S(1)}, bf16[1,4,128,128]{3,2,1,0:T(8,128)(2,1)S(1)}, u32[]{:S(2)}, u32[]{:S(2)}) collective-permute-start(bf16[1,4,128,128]{3,2,1,0:T(8,128)(2,1)S(1)} %collective-permute-done.9), channel_id=1, source_target_pairs={{0,30},{2,0},{4,2},{6,4},{8,6},{10,8},{12,10},{14,12},{16,14},{18,... | collective-permute-start | bytes 393224 | tf_op jit(solution)/shard_map/ppermute | solution.py:19
  240.4 8.7 %collective-permute-start.12 = (bf16[1,4,128,128]{3,2,1,0:T(8,128)(2,1)S(1)}, bf16[1,4,128,128]{3,2,1,0:T(8,128)(2,1)S(1)}, u32[]{:S(2)}, u32[]{:S(2)}) collective-permute-start(bf16[1,4,128,128]{3,2,1,0:T(8,128)(2,1)S(1)} %collective-permute-done.10), channel_id=1, source_target_pairs={{0,2},{2,4},{4,6},{6,8},{8,10},{10,12},{12,14},{14,16},{16,18},{18... | collective-permute-start | bytes 393224 | tf_op jit(solution)/shard_map/ppermute | solution.py:16
  240.4 8.7 %collective-permute-start.13 = (bf16[1,4,128,128]{3,2,1,0:T(8,128)(2,1)S(1)}, bf16[1,4,128,128]{3,2,1,0:T(8,128)(2,1)S(1)}, u32[]{:S(2)}, u32[]{:S(2)}) collective-permute-start(bf16[1,4,128,128]{3,2,1,0:T(8,128)(2,1)S(1)} %collective-permute-done.11), channel_id=1, source_target_pairs={{0,30},{2,0},{4,2},{6,4},{8,6},{10,8},{12,10},{14,12},{16,14},{18,... | collective-permute-start | bytes 393224 | tf_op jit(solution)/shard_map/ppermute | solution.py:19
  249.1 8.6 %collective-permute-start.14 = (bf16[1,4,128,128]{3,2,1,0:T(8,128)(2,1)S(1)}, bf16[1,4,128,128]{3,2,1,0:T(8,128)(2,1)S(1)}, u32[]{:S(2)}, u32[]{:S(2)}) collective-permute-start(bf16[1,4,128,128]{3,2,1,0:T(8,128)(2,1)S(1)} %collective-permute-done.12), channel_id=1, source_target_pairs={{0,2},{2,4},{4,6},{6,8},{8,10},{10,12},{12,14},{14,16},{16,18},{18... | collective-permute-start | bytes 393224 | tf_op jit(solution)/shard_map/ppermute | solution.py:16
Sparse Core Ops, SparseCore 0:
  13.5 144.4 all-reduce.1
